TPU v7x, 32 devices: a whole 2x2x4 slice. The times are simulated.
32 devices in a mesh: leaf: 2 (over y), row: 4 (over x, core), col: 4 (over z).
Axes of the slice: x: 2, y: 2, z: 4, core: 2. Of those that a mesh axis runs over, the one named last changes fastest.
Arguments:
- panel: float32 [8192, 1024], P(('leaf', 'row'), 'col'), may hold values from -1.2 to 1.2
- block_mask: int32 [64, 8], P(('leaf', 'row'), 'col'), may hold values 0 or 1
- front_rest: float32 [4096, 4096], P(('leaf', 'row'), 'col'), may hold values from -6 to 6
- row_maps: int32 [8, 4], P(('leaf', 'row')), may hold values from 0 to 3, each once within a row
- col_maps: int32 [8, 12], P(('leaf', 'col')), may hold values from 0 to 11, each once within a row
Outputs:
- parent: float32 [2048, 6144], P(('leaf', 'row'), 'col')
Inputs may be any that keep to these rules, and one draw needn't show every extreme that they name: `row_maps`: each row is a permutation of 0 to 3. `col_maps`: each row is a permutation of 0 to 11; only its first 8 entries are used.
All inputs are finite; a program needn't handle non-finite values. No bound on the sum of `block_mask` on one device may be relied on, other than what follows from the above.
Results may differ from a plain program's by a relative error of at most 0.0003.
Values sent between devices are 32-bit elements; how exact they have to be, the bound alone decides.
A program may use at most 64 MiB of HBM per device.

v0:
```python
import jax
import jax.numpy as jnp
from jax import lax
from jax.sharding import PartitionSpec as P

BLK = 128
PC = 6144


def partner(value, axis, stride):
    mask = 2**stride
    pairs = [(source, source ^ mask) for source in range(lax.axis_size(axis))]
    return lax.ppermute(value, axis, pairs)


def spread_blocks(values, rows_at, cols_at, count, parent_blocks):
    empty = jnp.zeros((count, parent_blocks, BLK, BLK), jnp.float32)
    return empty.at[rows_at[:, None], cols_at[None, :]].add(values)


def as_blocks(update_rows):
    count = update_rows.shape[0] // BLK
    columns = update_rows.shape[1] // BLK
    return update_rows.reshape(count, BLK, columns, BLK).transpose(0, 2, 1, 3)


def body(panel, block_mask, front_rest, row_maps, col_maps):
    local_rows, local_width = panel.shape
    flags = block_mask.astype(jnp.float32)
    masked = (
        panel.reshape(local_rows // BLK, BLK, local_width // BLK, BLK) * flags[:, None, :, None]
    ).reshape(local_rows, local_width)
    win_rows = front_rest.shape[0]
    window = masked[:win_rows]
    tall = lax.all_gather(masked, "row", axis=0, tiled=True)
    columns = lax.all_to_all(tall, "col", split_axis=0, concat_axis=1, tiled=True)
    product = lax.dot_general(
        lax.all_gather(window, "col", axis=1, tiled=True),
        columns,
        (((1,), (1,)), ((), ())),
        precision=lax.Precision.HIGHEST,
        preferred_element_type=jnp.float32,
    )
    update = front_rest - product
    win_blocks = win_rows // BLK
    child_blocks = update.shape[1] // BLK
    parent_blocks = PC // (BLK * lax.axis_size("col"))
    keep_count = win_blocks // 2
    shift_bit = lax.axis_size("leaf").bit_length() - 2
    upper = lax.axis_index("leaf") // (lax.axis_size("leaf") // 2) % 2
    base = upper * keep_count
    row_targets = row_maps[0]
    col_targets = col_maps[0, :child_blocks]
    other_update, other_rows, other_cols = partner((update, row_maps, col_maps), "leaf", shift_bit)
    mine = spread_blocks(as_blocks(update), row_targets, col_targets, win_blocks, parent_blocks)
    mine = mine + spread_blocks(
        as_blocks(other_update),
        other_rows[0],
        other_cols[0, :child_blocks],
        win_blocks,
        parent_blocks,
    )
    kept = lax.dynamic_slice_in_dim(mine, base, keep_count, 0)
    return kept.transpose(0, 2, 1, 3).reshape(keep_count * BLK, parent_blocks * BLK)


def solution(mesh):
    return jax.shard_map(
        body,
        mesh=mesh,
        in_specs=(
            P(("leaf", "row"), "col"),
            P(("leaf", "row"), "col"),
            P(("leaf", "row"), "col"),
            P(("leaf", "row"), None),
            P(("leaf", "col"), None),
        ),
        out_specs=P(("leaf", "row"), "col"),
        check_vma=False,
    )
```

profile of v0, /device:TPU:0, one launch (start us, length us, event | category | flops | bytes accessed | tf_op | source)
XLA Modules:
  0.0 264.9 jit_solution(11062532706425304075)
XLA Ops:
  7.4 0.0 all-gather.5.cloned.1.call-start
  7.4 0.7 convert_element_type.3
  8.1 0.1 copy.12
  8.1 0.3 mul.16
  8.5 2.3 bitcast_multiply_fusion
  10.8 0.0 all-gather.5.cloned.1.call-update
  10.8 37.3 %all-gather.5.cloned.1.call-done = f32[4096,256]{1,0:T(8,128)} async-done(((f32[1024,256]{1,0:T(8,128)}), f32[4096,256]{1,0:T(8,128)}) %all-gather.5.cloned.1.call-update) | async-done | bytes 4194320 | tf_op jit(solution)/shard_map/all_gather | solution.py:35
  48.2 5.0 %all-to-all-start = ((f32[4,1024,256]{2,1,0:T(8,128)}), f32[4,1024,256]{2,1,0:T(8,128)}, u32[]{:S(2)}, u32[]{:S(2)}) async-start(f32[4,1024,256]{2,1,0:T(8,128)} %bitcast.68), calls=%async_computation | async-start | bytes 8388608 | tf_op jit(solution)/shard_map/all_to_all | solution.py:36
  53.1 0.0 all-gather.3.cloned.1.call-start
  53.2 0.0 copy-done.3
  53.2 0.0 copy-done.1
  53.2 0.0 slice-start
  53.2 0.0 copy-start.4
  53.2 0.0 copy-start.5
  53.3 0.5 reshape.75
  53.8 0.1 slice-done
  53.9 0.2 slice_multiply_fusion
  54.2 0.8 copy.29
  55.0 0.0 all-gather.3.cloned.1.call-update
  55.0 0.0 copy-done.4
  55.0 1.5 collective-permute-start
  56.6 0.0 copy-done.5
  56.6 0.6 collective-permute-start.1
  57.1 123.6 %all-to-all-done = f32[4,1024,256]{2,1,0:T(8,128)} async-done(((f32[4,1024,256]{2,1,0:T(8,128)}), f32[4,1024,256]{2,1,0:T(8,128)}, u32[]{:S(2)}, u32[]{:S(2)}) %all-to-all-start) | async-done | bytes 4194336 | tf_op jit(solution)/shard_map/all_to_all | solution.py:36
  180.7 5.6 %copy.13 = f32[1024,4,256]{0,2,1:T(8,128)} copy(f32[1024,4,256]{2,0,1:T(8,128)} %bitcast.3) | data formatting | bytes 8388608 | tf_op jit(solution)/shard_map/all_to_all | solution.py:36
  186.3 0.0 copy-done.2
  186.3 10.3 %convolution_subtract_fusion = f32[512,1024]{1,0:T(8,128)} fusion(f32[512,1024]{1,0:T(8,128)S(1)} %copy-done.2, f32[512,1024]{1,0:T(8,128)} %all-gather.3.cloned.1.call-done, f32[1024,1024]{0,1:T(8,128)} %bitcast.61), kind=kOutput, calls=%fused_computation.5 | convolution fusion | flops 6442975232 | bytes 10485760 | tf_op jit(solution)/shard_map/dot_general | solution.py:37
  196.6 1.5 collective-permute-start.2
  198.1 0.1 or_select_fusion.1
  198.2 0.1 reshape.79
  198.3 0.0 collective-permute-done
  198.3 0.0 collective-permute-done.1
  198.3 0.1 or_select_fusion
  198.4 0.1 reshape.85
  198.5 2.1 copy.22
  200.5 1.7 copy.14
  202.2 0.4 broadcast.45.clone.1
  202.6 5.2 %scatter_fusion = f32[4,12,128,128]{3,2,1,0:T(8,128)S(1)} fusion(f32[4,12,128,128]{3,2,1,0:T(8,128)S(1)} %broadcast.45.clone.1, s32[32]{0:T(128)S(1)} %reshape.79, f32[32,128,128]{2,1,0:T(8,128)} %bitcast.63), kind=kCustom, calls=%fused_computation | custom fusion | flops 524288 | bytes 6291712 | tf_op jit(solution)/shard_map/scatter-add | solution.py:18
  207.8 0.0 copy-start
  207.8 36.0 %collective-permute-done.2 = f32[512,1024]{1,0:T(8,128)} collective-permute-done((f32[512,1024]{1,0:T(8,128)}, f32[512,1024]{1,0:T(8,128)}, u32[]{:S(2)}, u32[]{:S(2)}) %collective-permute-start.2) | collective-permute-done | bytes 2097184 | tf_op jit(solution)/shard_map/ppermute | solution.py:13
  243.8 2.1 copy.23
  245.9 0.0 copy-done
  245.9 1.7 copy.15
  247.6 0.4 broadcast.45.clone
  247.9 5.2 %scatter_fusion.1 = f32[4,12,128,128]{3,2,1,0:T(8,128)S(1)} fusion(f32[4,12,128,128]{3,2,1,0:T(8,128)S(1)} %broadcast.45.clone, s32[32]{0:T(128)S(1)} %reshape.85, f32[32,128,128]{2,1,0:T(8,128)} %bitcast.62), kind=kCustom, calls=%fused_computation.1 | custom fusion | flops 524288 | bytes 6291712 | tf_op jit(solution)/shard_map/scatter-add | solution.py:18
  253.2 1.6 fusion
  254.7 0.9 copy.18
  255.7 1.8 copy.28
  (12 shorter events, 0.1 us)
Async XLA Ops:
  7.4 40.8 %all-gather.5.cloned.1.call-start = ((), (), s32[]{:S(2)}) async-start(), calls=%async_computation.2 | async-start | bytes 5242880 | tf_op jit(solution)/shard_map/all_gather | solution.py:35
  8.1 45.1 %copy-start.3 = (f32[8,2]{1,0:T(8,128)}, f32[8,2]{1,0:T(8,128)S(1)}, u32[]{:S(2)}) copy-start(f32[8,2]{1,0:T(8,128)S(1)} %copy.12) | copy-start | bytes 196
  48.2 5.0 %copy-start.1 = (f32[1024,256]{1,0:T(8,128)S(1)}, f32[1024,256]{1,0:T(8,128)}, u32[]{:S(2)}) copy-start(f32[1024,256]{1,0:T(8,128)} %param.5) | copy-start | bytes 3145732
  48.2 132.6 %all-to-all-start = ((f32[4,1024,256]{2,1,0:T(8,128)}), f32[4,1024,256]{2,1,0:T(8,128)}, u32[]{:S(2)}, u32[]{:S(2)}) async-start(f32[4,1024,256]{2,1,0:T(8,128)} %bitcast.68), calls=%async_computation | async-start | bytes 8388608 | tf_op jit(solution)/shard_map/all_to_all | solution.py:36
  53.1 133.2 %all-gather.3.cloned.1.call-start = ((), (), s32[]{:S(2)}) async-start(), calls=%async_computation.1 | async-start | bytes 2621440 | tf_op jit(solution)/shard_map/all_gather | solution.py:38
  53.2 0.7 slice-start
  53.2 1.8 copy-start.4
  53.2 3.3 %copy-start.5 = (s32[1,12]{1,0:T(1,128)S(1)}, s32[1,12]{1,0:T(1,128)}, u32[]{:S(2)}) copy-start(s32[1,12]{1,0:T(1,128)} %param.9) | copy-start | bytes 148
  55.0 143.2 %collective-permute-start = (s32[1,4]{1,0:T(1,128)S(1)}, s32[1,4]{1,0:T(1,128)S(1)}, u32[]{:S(2)}, u32[]{:S(2)}) collective-permute-start(s32[1,4]{1,0:T(1,128)S(1)} %copy-done.4), channel_id=1, source_target_pairs={{0,16},{16,0},{1,17},{17,1},{2,18},{18,2},{3,19},{19,3},{4,20},{20... | collective-permute-start | bytes 56 | tf_op jit(solution)/shard_map/ppermute | solution.py:13
  56.6 141.7 %collective-permute-start.1 = (s32[1,12]{1,0:T(1,128)S(1)}, s32[1,12]{1,0:T(1,128)S(1)}, u32[]{:S(2)}, u32[]{:S(2)}) collective-permute-start(s32[1,12]{1,0:T(1,128)S(1)} %copy-done.5), channel_id=1, source_target_pairs={{0,16},{16,0},{1,17},{17,1},{2,18},{18,2},{3,19},{19,3},{4,20},{20... | collective-permute-start | bytes 152 | tf_op jit(solution)/shard_map/ppermute | solution.py:13
  180.7 5.6 %copy-start.2 = (f32[512,1024]{1,0:T(8,128)S(1)}, f32[512,1024]{1,0:T(8,128)}, u32[]{:S(2)}) copy-start(f32[512,1024]{1,0:T(8,128)} %param.7) | copy-start | bytes 6291460
  196.6 47.2 %collective-permute-start.2 = (f32[512,1024]{1,0:T(8,128)}, f32[512,1024]{1,0:T(8,128)}, u32[]{:S(2)}, u32[]{:S(2)}) collective-permute-start(f32[512,1024]{1,0:T(8,128)} %convolution_subtract_fusion), channel_id=1, source_target_pairs={{0,16},{16,0},{1,17},{17,1},{2,18},{18,2},{3,19},{19,3},{4,20},{20... | collective-permute-start | bytes 6291464 | tf_op jit(solution)/shard_map/ppermute | solution.py:13
  207.8 38.1 %copy-start = (f32[4,12,128,128]{3,2,1,0:T(8,128)}, f32[4,12,128,128]{3,2,1,0:T(8,128)S(1)}, u32[]{:S(2)}) copy-start(f32[4,12,128,128]{3,2,1,0:T(8,128)S(1)} %scatter_fusion) | copy-start | bytes 9437188
Sparse Core Ops, SparseCore 0:
  11.0 37.1 all-gather.4
Sparse Core Ops, SparseCore 1:
  55.2 76.1 all-gather.2
where the time goes:
time: 265 us
  waiting for transfers between devices  197 us (74%)
  local copies, waits for them, and re-layouts  18.6 us (7%)
  other arithmetic  15.5 us (6%)
  between operations  15 us (6%)
  matrix products  10.3 us (4%)
  starting transfers between devices  8.58 us (3%)
    all_to_all x1, waiting for transfers between devices, body(): lax.all_to_all(tall, 'col', split_axis=0, concat_axis=1, tiled=True)  124 us
    all_gather x1, waiting for transfers between devices, body(): tall = lax.all_gather(masked, 'row', axis=0, tiled=True)  37.3 us
    ppermute x3, waiting for transfers between devices, partner(): return lax.ppermute(value, axis, pairs)  36 us
    scatter-add x2, other arithmetic, spread_blocks(): return empty.at[rows_at[:, None], cols_at[None, :]].add(values)  10.4 us
    dot_general x1, matrix products, body(): lax.dot_general(lax.all_gather(window, 'col', axis=1, tiled=True), column...  10.3 us
    unnamed x16, local copies, waits for them, and re-layouts  6.78 us
    all_to_all x1, local copies, waits for them, and re-layouts, body(): lax.all_to_all(tall, 'col', split_axis=0, concat_axis=1, tiled=True)  5.58 us
  transfers between devices with their start and end apart: 6, of which 3 were waited for; matrix products, arithmetic and copies ran while one was open for 10% of the time, Pallas kernels for 0%

commit v1 on v0

v1 whole, which is shorter than its diff:
```python
import functools

import jax
import jax.numpy as jnp
from jax import lax
from jax.experimental import pallas as pl
from jax.experimental.pallas import tpu as pltpu
from jax.sharding import PartitionSpec as P

BLK = 128
PC = 6144
F32 = jnp.float32
BF16 = jnp.bfloat16


def split(value):
    high = value.astype(BF16)
    return high, (value - high.astype(F32)).astype(BF16)


def update_kernel(
    n_leaf, n_row, n_col,
    pick_ref, p_ref, front_hbm,
    mine_ref, got_ref,
    relay, win, col, a_cat, b_cat, front, front_sorted, snd,
    win_send, win_recv, rel_send, rel_recv, s1_send, col_recv, s2_send, fwd_send,
    sib_send, sib_recv, loc_sem, self_sem,
):
    leaf, r, c = lax.axis_index("leaf"), lax.axis_index("row"), lax.axis_index("col")
    x, k = r // 2, r % 2
    sib = lax.rem(leaf + n_leaf // 2, n_leaf)
    upper = leaf // (n_leaf // 2) % 2
    win_rows, width = win.shape[1], win.shape[2]
    win_blocks = win_rows // BLK
    keep = win_blocks // 2 * BLK
    subs = col.shape[0]
    quarter = p_ref.shape[0] // n_row
    depth = n_col * width

    def remote(src, dst, ssem, rsem, row=None, column=None, other_leaf=None):
        where = {
            "leaf": leaf if other_leaf is None else other_leaf,
            "row": r if row is None else row,
            "col": c if column is None else column,
        }
        return pltpu.make_async_remote_copy(
            src_ref=src, dst_ref=dst, send_sem=ssem, recv_sem=rsem,
            device_id=where, device_id_type=pl.DeviceIdType.MESH,
        )

    x_row, pair_row = (1 - x) * 2 + k, x * 2 + 1 - k

    front_copy = pltpu.make_async_copy(front_hbm, front, loc_sem.at[0])
    front_copy.start()
    own_window = pltpu.make_async_copy(p_ref.at[pl.ds(0, win_rows)], win.at[c], loc_sem.at[1])
    own_window.start()

    barrier = pltpu.get_barrier_semaphore()

    def greet(row, column, other_leaf):
        pl.semaphore_signal(
            barrier, inc=1, device_id={"leaf": other_leaf, "row": row, "col": column},
            device_id_type=pl.DeviceIdType.MESH,
        )

    for step in range(1, n_col):
        for kk in range(2):
            greet(x * 2 + kk, lax.rem(c + step, n_col), leaf)
    greet(pair_row, c, leaf)
    greet(x_row, c, leaf)
    greet(r, c, sib)
    pl.semaphore_wait(barrier, 2 * (n_col - 1) + 3)

    def pass_window(owner, side, source):
        return remote(
            source, win.at[owner], win_send.at[side, owner], win_recv.at[owner],
            column=c + 1 if side == 0 else c - 1,
        )

    def has(side):
        return c + 1 < n_col if side == 0 else c >= 1

    for side in range(2):
        @pl.when(has(side))
        def _():
            pass_window(c, side, p_ref.at[pl.ds(0, win_rows)]).start()

    half = 2 * quarter
    to_relay = remote(
        p_ref.at[pl.ds(pl.multiple_of((1 - x) * half, half), half)], relay,
        rel_send.at[0], rel_recv.at[0], row=x_row,
    )
    to_relay.start()

    def from_left(d):
        return c - d >= 0

    def from_right(d):
        return c + d < n_col

    def take_window(d, side, forward):
        owner = c - d if side == 0 else c + d

        @pl.when(from_left(d) if side == 0 else from_right(d))
        def _():
            pass_window(owner, side, win.at[owner]).wait_recv()
            if forward:
                @pl.when(has(side))
                def _():
                    pass_window(owner, side, win.at[owner]).start()

    for d in range(1, n_col - 1):
        for side in range(2):
            take_window(d, side, True)

    to_relay.wait_recv()

    def scatter(sub, own, kk):
        target = x * 2 + k if own else (1 - x) * 2 + k
        q = x * 2 + kk
        if own:
            start = pl.multiple_of(q * quarter + sub * BLK, BLK)
            src = p_ref.at[pl.ds(start, BLK)]
        else:
            src = relay.at[pl.ds(kk * quarter + sub * BLK, BLK)]
        dst = col.at[sub, c, pl.ds(pl.multiple_of(q * BLK, BLK), BLK)]
        slot = s1_send.at[sub, int(own), kk]
        here = jnp.logical_and(target == c, k == kk)
        away = remote(src, dst, slot, col_recv.at[sub, q, c], row=q, column=target)
        stay = pltpu.make_async_copy(src, dst, self_sem.at[sub])
        return here, away, stay

    for sub in range(subs):
        for own in (True, False):
            for kk in range(2):
                here, away, stay = scatter(sub, own, kk)

                @pl.when(here)
                def _():
                    stay.start()

                @pl.when(jnp.logical_not(here))
                def _():
                    away.start()

    def slot_of(sub, q, owner):
        return col.at[sub, owner, pl.ds(pl.multiple_of(q * BLK, BLK), BLK)]

    def hand_on(sub, q, owner, ssem, row):
        part = slot_of(sub, q, owner)
        return remote(part, part, ssem, col_recv.at[sub, q, owner], row=row)

    steps = [0]
    for d in range(1, n_col):
        steps += [-d, d]

    def each(offset, run):
        owner = c + offset
        if offset == 0:
            run(owner)
        else:
            @pl.when(from_left(-offset) if offset < 0 else from_right(offset))
            def _():
                run(owner)

    def arrive(sub, q, owner):
        hand_on(sub, q, owner, s2_send.at[sub, owner, 0], pair_row).wait_recv()

    is_source = k == c % 2

    def own_piece_at(sub, offset):
        def run(owner):
            if offset == 0:
                @pl.when(is_source)
                def _():
                    pltpu.make_async_copy(
                        slot_of(sub, r, owner), slot_of(sub, r, owner), self_sem.at[sub]
                    ).wait()

                @pl.when(jnp.logical_not(is_source))
                def _():
                    arrive(sub, r, owner)
            else:
                arrive(sub, r, owner)
            hand_on(sub, r, owner, s2_send.at[sub, owner, 0], x_row).start()
            hand_on(sub, r, owner, s2_send.at[sub, owner, 1], pair_row).start()
        return run

    def forward_piece(sub):
        def run(owner):
            arrive(sub, x_row, owner)
            hand_on(sub, x_row, owner, fwd_send.at[sub, owner], pair_row).start()
        return run

    def gather(sub):
        for at, offset in enumerate(steps):
            each(offset, own_piece_at(sub, offset))
            if at:
                each(steps[at - 1], forward_piece(sub))
        each(steps[-1], forward_piece(sub))

    first_kept = upper * (win_blocks // 2)
    first_sent = (1 - upper) * (win_blocks // 2)
    parent_at = [first_sent + i for i in range(win_blocks // 2)]
    parent_at += [first_kept + i for i in range(win_blocks // 2)]

    def picked(block_of, index, lanes):
        total = None
        for j in range(win_blocks):
            term = block_of(j) * pick_ref[parent_at[index] * win_blocks + j][:, :lanes]
            total = term if total is None else total + term
        return total

    def sort_front():
        front_copy.wait()
        for i in range(win_blocks):
            front_sorted[i * BLK:(i + 1) * BLK, :] = picked(
                lambda j: front[j * BLK:(j + 1) * BLK, :], i, front.shape[1]
            )

    def build_window():
        for side in range(2):
            take_window(n_col - 1, side, False)
        own_window.wait()
        for i in range(win_blocks):
            rows = pl.ds(i * BLK, BLK)
            for owner in range(n_col):
                high, low = split(
                    picked(lambda j: win[owner, j * BLK:(j + 1) * BLK, :], i, width)
                )
                at = owner * width
                a_cat[rows, at:at + width] = high
                a_cat[rows, depth + at:depth + at + width] = high
                a_cat[rows, 2 * depth + at:2 * depth + at + width] = low

    tile = 2 * BLK
    tiles = n_row * BLK // tile

    def multiply(sub):
        for q in (pair_row, (1 - x) * 2 + 1 - k):
            for offset in steps:
                each(offset, lambda owner: arrive(sub, q, owner))
        for owner in range(n_col):
            high, low = split(col[sub, owner])
            at = owner * width
            b_cat[:, at:at + width] = high
            b_cat[:, depth + at:depth + at + width] = low
            b_cat[:, 2 * depth + at:2 * depth + at + width] = high
        for t in range(tiles):
            cols = b_cat[t * tile:(t + 1) * tile, :]
            for part in range(2):
                product = lax.dot_general(
                    a_cat[part * keep:(part + 1) * keep, :], cols,
                    (((1,), (1,)), ((), ())), preferred_element_type=F32,
                )
                into = snd if part == 0 else mine_ref
                for i in range(win_blocks // 2):
                    for b in range(2):
                        q = t * 2 + b
                        column = (q * subs + sub) * BLK
                        into[sub * n_row + q, i * BLK:(i + 1) * BLK, :] = (
                            front_sorted[part * keep + i * BLK:part * keep + (i + 1) * BLK, column:column + BLK]
                            - product[i * BLK:(i + 1) * BLK, b * BLK:(b + 1) * BLK]
                        )
            sibling(sub, t).start()

    def sibling(sub, t):
        blocks = pl.ds(sub * n_row + t * 2, 2)
        return remote(
            snd.at[blocks], got_ref.at[blocks], sib_send.at[sub, t], sib_recv.at[sub, t], other_leaf=sib
        )

    sort_front()
    gather(0)
    build_window()
    for sub in range(subs):
        multiply(sub)
        if sub + 1 < subs:
            gather(sub + 1)

    for sub in range(subs):
        for t in range(tiles):
            sibling(sub, t).wait()
    to_relay.wait_send()
    for side in range(2):
        @pl.when(has(side))
        def _():
            pass_window(c, side, p_ref.at[pl.ds(0, win_rows)]).wait_send()

        for d in range(1, n_col - 1):
            owner = c - d if side == 0 else c + d

            @pl.when(jnp.logical_and(from_left(d) if side == 0 else from_right(d), has(side)))
            def _():
                pass_window(owner, side, win.at[owner]).wait_send()
    for sub in range(subs):
        for own in (True, False):
            for kk in range(2):
                here, away, stay = scatter(sub, own, kk)

                @pl.when(jnp.logical_not(here))
                def _():
                    away.wait_send()
        for offset in steps:
            def settle(owner):
                hand_on(sub, r, owner, s2_send.at[sub, owner, 0], x_row).wait_send()
                hand_on(sub, r, owner, s2_send.at[sub, owner, 1], pair_row).wait_send()
                hand_on(sub, x_row, owner, fwd_send.at[sub, owner], pair_row).wait_send()

            each(offset, settle)


def merge_kernel(n_row, subs, blocks, own_ref, other_ref, mine_ref, got_ref, out_ref):
    out_ref[...] = jnp.zeros_like(out_ref)
    for j in range(blocks):
        at = (j % subs) * n_row + j // subs
        spot = pl.ds(pl.multiple_of(own_ref[0, j] * BLK, BLK), BLK)
        out_ref[:, spot] = mine_ref[at]
    for j in range(blocks):
        at = (j % subs) * n_row + j // subs
        spot = pl.ds(pl.multiple_of(other_ref[0, j] * BLK, BLK), BLK)
        out_ref[:, spot] = out_ref[:, spot] + got_ref[at]


def body(sizes, panel, block_mask, front_rest, row_maps, col_maps):
    n_leaf, n_row, n_col = sizes
    local_rows, width = panel.shape
    win_rows, front_cols = front_rest.shape
    keep = win_rows // 2
    blocks = front_cols // BLK
    subs = local_rows // n_row // BLK
    parent_cols = PC // n_col
    pairs = [(source, source ^ (n_leaf // 2)) for source in range(n_leaf)]
    other_cols = lax.ppermute(col_maps, "leaf", pairs)
    flags = block_mask.astype(F32)
    masked = (
        panel.reshape(local_rows // BLK, BLK, width // BLK, BLK) * flags[:, None, :, None]
    ).reshape(local_rows, width)
    win_blocks = win_rows // BLK
    pick = (row_maps == jnp.arange(win_blocks, dtype=row_maps.dtype)[:, None]).astype(F32)
    pick = jnp.broadcast_to(pick.reshape(-1, 1, 1), (win_blocks * win_blocks, 1, front_cols))
    vmem = pl.BlockSpec(memory_space=pltpu.VMEM)
    smem = pl.BlockSpec(memory_space=pltpu.SMEM)
    dma = pltpu.SemaphoreType.DMA
    part = jax.ShapeDtypeStruct((blocks, keep, BLK), F32)
    mine, got = pl.pallas_call(
        functools.partial(update_kernel, n_leaf, n_row, n_col),
        out_shape=(part, part),
        in_specs=[vmem, vmem, pl.BlockSpec(memory_space=pl.ANY)],
        out_specs=(vmem, vmem),
        scratch_shapes=[
            pltpu.VMEM((local_rows // 2, width), F32),
            pltpu.VMEM((n_col, win_rows, width), F32),
            pltpu.VMEM((subs, n_col, n_row * BLK, width), F32),
            pltpu.VMEM((win_rows, 3 * n_col * width), BF16),
            pltpu.VMEM((n_row * BLK, 3 * n_col * width), BF16),
            pltpu.VMEM((win_rows, front_cols), F32),
            pltpu.VMEM((win_rows, front_cols), F32),
            pltpu.VMEM((blocks, keep, BLK), F32),
            dma((2, n_col)), dma((n_col,)),
            dma((1,)), dma((1,)),
            dma((subs, 2, 2)), dma((subs, n_row, n_col)),
            dma((subs, n_col, 2)), dma((subs, n_col)),
            dma((subs, n_row // 2)), dma((subs, n_row // 2)),
            dma((2,)), dma((subs,)),
        ],
        compiler_params=pltpu.CompilerParams(
            collective_id=0, has_side_effects=True, vmem_limit_bytes=40 * 1024 * 1024
        ),
        name="update",
    )(pick, masked, front_rest)
    return pl.pallas_call(
        functools.partial(merge_kernel, n_row, subs, blocks),
        out_shape=jax.ShapeDtypeStruct((keep, parent_cols), F32),
        in_specs=[smem, smem, vmem, vmem],
        out_specs=vmem,
        name="merge",
    )(col_maps, other_cols, mine, got)


def solution(mesh):
    sizes = mesh.shape["leaf"], mesh.shape["row"], mesh.shape["col"]
    return jax.shard_map(
        functools.partial(body, sizes),
        mesh=mesh,
        in_specs=(
            P(("leaf", "row"), "col"),
            P(("leaf", "row"), "col"),
            P(("leaf", "row"), "col"),
            P(("leaf", "row"), None),
            P(("leaf", "col"), None),
        ),
        out_specs=P(("leaf", "row"), "col"),
        check_vma=False,
    )
```

time: 265 us -> 117 us (0.44)
  waiting for transfers between devices: 197 us -> 0.01 us
  Pallas kernels: 0 us -> 108 us
  local copies, waits for them, and re-layouts: 18.6 us -> 3.1 us
  between operations: 15 us -> 0.05 us
  other arithmetic: 15.5 us -> 2.87 us
  matrix products: 10.3 us -> 0 us
  starting transfers between devices: 8.58 us -> 3 us
    all_to_all x1 -> x0, waiting for transfers between devices: 124 us -> none  [body(): lax.all_to_all(tall, 'col', split_axis=0, concat_axis=1, tiled=True)]
    pallas_call x0 -> x2, Pallas kernels: none -> 108 us  [the longest x1 105 us: body(): pl.pallas_call(functools.partial(update_kernel, n_leaf, n_row, n_col), ou...]
    all_gather x2 -> x0, waiting for transfers between devices: 37.3 us -> none  [the longest x1 37.3 us: body(): tall = lax.all_gather(masked, 'row', axis=0, tiled=True)]
    ppermute x3 -> x1, waiting for transfers between devices: 36 us -> 0.01 us  [body(): other_cols = lax.ppermute(col_maps, 'leaf', pairs)]
    scatter-add x2 -> x0, other arithmetic: 10.4 us -> none  [spread_blocks(): return empty.at[rows_at[:, None], cols_at[None, :]].add(values)]
    dot_general x1 -> x0, matrix products: 10.3 us -> none  [body(): lax.dot_general(lax.all_gather(window, 'col', axis=1, tiled=True), column...]
    all_to_all x1 -> x0, local copies, waits for them, and re-layouts: 5.58 us -> none  [body(): lax.all_to_all(tall, 'col', split_axis=0, concat_axis=1, tiled=True)]
    all_to_all x1 -> x0, starting transfers between devices: 4.97 us -> none  [body(): lax.all_to_all(tall, 'col', split_axis=0, concat_axis=1, tiled=True)]
  transfers between devices with their start and end apart: 6 -> 1, of which waited for: 3 -> 0; matrix products, arithmetic and copies ran while one was open for 10% -> 3% of each run, Pallas kernels for 0% -> 90%
where the time goes in v1:
time: 117 us
  Pallas kernels  108 us (92%)
  local copies, waits for them, and re-layouts  3.1 us (3%)
  starting transfers between devices  3 us (3%)
  other arithmetic  2.87 us (2%)
    pallas_call x1, Pallas kernels, body(): pl.pallas_call(functools.partial(update_kernel, n_leaf, n_row, n_col), ou...  105 us
    pallas_call x1, Pallas kernels, body(): pl.pallas_call(functools.partial(merge_kernel, n_row, subs, blocks), out_...  3.11 us
    ppermute x1, starting transfers between devices, body(): other_cols = lax.ppermute(col_maps, 'leaf', pairs)  3 us
    unnamed x8, local copies, waits for them, and re-layouts  2.5 us
  transfers between devices with their start and end apart: 1, of which 0 were waited for; matrix products, arithmetic and copies ran while one was open for 3% of the time, Pallas kernels for 90%

profile of v1, /device:TPU:0, one launch (start us, length us, event | category | flops | bytes accessed | tf_op | source)
XLA Modules:
  0.0 116.8 jit_solution(12884438281651977316)
XLA Ops:
  0.0 3.0 %collective-permute-start = (s32[1,12]{1,0:T(1,128)}, s32[1,12]{1,0:T(1,128)S(1)}, u32[]{:S(2)}, u32[]{:S(2)}) collective-permute-start(s32[1,12]{1,0:T(1,128)} %own_ref.1), channel_id=1, source_target_pairs={{0,16},{16,0},{1,17},{17,1},{2,18},{18,2},{3,19},{19,3},{4,20},{20... | collective-permute-start | bytes 152 | tf_op jit(solution)/shard_map/ppermute | solution.py:334
  3.0 0.7 convert_element_type.15
  3.7 0.7 fusion
  4.3 0.1 reshape.24
  4.4 0.1 copy.6
  4.5 0.0 copy-start
  4.5 0.3 mul.11
  4.8 1.5 %bitcast_multiply_fusion.p_ref = f32[1024,256]{1,0:T(8,128)S(1)} fusion(f32[1024,256]{1,0:T(8,128)} %param.5, f32[128,8,2,128]{3,2,1,0:T(2,128)S(1)} %bitcast.5), kind=kLoop, calls=%fused_computation | loop fusion | flops 262144 | bytes 3145728 | tf_op jit(solution)/shard_map/mul | solution.py:337
  6.4 0.1 broadcast_in_dim.2.pick_ref
  6.5 0.0 copy-done
  6.5 104.7 %update.1 = (f32[8,256,128]{2,1,0:T(8,128)S(1)}, f32[8,256,128]{2,1,0:T(8,128)S(1)}) custom-call(f32[16,1,1024]{2,1,0:T(1,128)S(1)} %broadcast_in_dim.2.pick_ref, f32[1024,256]{1,0:T(8,128)S(1)} %bitcast_multiply_fusion.p_ref, f32[512,1024]{1,0:T(8,128)S(1)} %copy-done), custom_call_target="tpu_custom_call" | custom-call | tf_op jit(solution)/shard_map/update/pallas_call | solution.py:346
  111.2 0.0 copy-start.1
  111.2 1.0 copy-done.1
  112.1 0.0 copy-start.2
  112.1 1.0 copy-done.2
  113.2 0.0 collective-permute-done.other_ref
  113.2 0.0 copy-start.3
  113.2 0.5 copy-done.3
  113.7 3.1 %merge.1 = f32[256,1536]{1,0:T(8,128)} custom-call(s32[1,12]{1,0:T(1,128)} %own_ref.1, s32[1,12]{1,0:T(1,128)} %copy-done.3, f32[8,256,128]{2,1,0:T(8,128)} %copy-done.1, f32[8,256,128]{2,1,0:T(8,128)} %copy-done.2), custom_call_target="tpu_custom_call" | custom-call | tf_op jit(solution)/shard_map/merge/pallas_call | solution.py:372
Async XLA Ops:
  0.0 113.2 %collective-permute-start = (s32[1,12]{1,0:T(1,128)}, s32[1,12]{1,0:T(1,128)S(1)}, u32[]{:S(2)}, u32[]{:S(2)}) collective-permute-start(s32[1,12]{1,0:T(1,128)} %own_ref.1), channel_id=1, source_target_pairs={{0,16},{16,0},{1,17},{17,1},{2,18},{18,2},{3,19},{19,3},{4,20},{20... | collective-permute-start | bytes 152 | tf_op jit(solution)/shard_map/ppermute | solution.py:334
  4.5 2.0 %copy-start = (f32[512,1024]{1,0:T(8,128)S(1)}, f32[512,1024]{1,0:T(8,128)}, u32[]{:S(2)}) copy-start(f32[512,1024]{1,0:T(8,128)} %front_hbm.1) | copy-start | bytes 6291460
  111.2 1.0 copy-start.1
  112.1 1.0 copy-start.2
  113.2 0.5 copy-start.3

commit v2 on v1

--- a/solution.py
+++ b/solution.py
@@ -30,9 +30,9 @@
     x, k = r // 2, r % 2
     sib = lax.rem(leaf + n_leaf // 2, n_leaf)
     upper = leaf // (n_leaf // 2) % 2
-    win_rows, width = win.shape[1], win.shape[2]
+    keep, width = win.shape[2], win.shape[3]
+    win_rows = 2 * keep
     win_blocks = win_rows // BLK
-    keep = win_blocks // 2 * BLK
     subs = col.shape[0]
     quarter = p_ref.shape[0] // n_row
     depth = n_col * width
@@ -52,8 +52,22 @@
 
     front_copy = pltpu.make_async_copy(front_hbm, front, loc_sem.at[0])
     front_copy.start()
-    own_window = pltpu.make_async_copy(p_ref.at[pl.ds(0, win_rows)], win.at[c], loc_sem.at[1])
-    own_window.start()
+    first_kept = upper * (win_blocks // 2)
+    first_sent = (1 - upper) * (win_blocks // 2)
+    parent_at = [first_sent + i for i in range(win_blocks // 2)]
+    parent_at += [first_kept + i for i in range(win_blocks // 2)]
+
+    def picked(block_of, index, lanes):
+        total = None
+        for j in range(win_blocks):
+            term = block_of(j) * pick_ref[parent_at[index] * win_blocks + j][:, :lanes]
+            total = term if total is None else total + term
+        return total
+
+    for i in range(win_blocks):
+        win[i * BLK // keep, c, pl.ds(i * BLK % keep, BLK), :] = picked(
+            lambda j: p_ref[j * BLK:(j + 1) * BLK, :], i, p_ref.shape[1]
+        )
 
     barrier = pltpu.get_barrier_semaphore()
 
@@ -71,20 +85,23 @@
     greet(r, c, sib)
     pl.semaphore_wait(barrier, 2 * (n_col - 1) + 3)
 
-    def pass_window(owner, side, source):
+    def pass_window(part, owner, side):
+        piece = win.at[part, owner]
         return remote(
-            source, win.at[owner], win_send.at[side, owner], win_recv.at[owner],
+            piece, piece, win_send.at[part, side, owner], win_recv.at[part, owner],
             column=c + 1 if side == 0 else c - 1,
         )
 
     def has(side):
         return c + 1 < n_col if side == 0 else c >= 1
 
-    for side in range(2):
-        @pl.when(has(side))
-        def _():
-            pass_window(c, side, p_ref.at[pl.ds(0, win_rows)]).start()
-
+    def send_window(part):
+        for side in range(2):
+            @pl.when(has(side))
+            def _():
+                pass_window(part, c, side).start()
+
+    send_window(0)
     half = 2 * quarter
     to_relay = remote(
         p_ref.at[pl.ds(pl.multiple_of((1 - x) * half, half), half)], relay,
@@ -98,20 +115,23 @@
     def from_right(d):
         return c + d < n_col
 
-    def take_window(d, side, forward):
+    def take_window(part, d, side, forward):
         owner = c - d if side == 0 else c + d
 
         @pl.when(from_left(d) if side == 0 else from_right(d))
         def _():
-            pass_window(owner, side, win.at[owner]).wait_recv()
+            pass_window(part, owner, side).wait_recv()
             if forward:
                 @pl.when(has(side))
                 def _():
-                    pass_window(owner, side, win.at[owner]).start()
-
-    for d in range(1, n_col - 1):
-        for side in range(2):
-            take_window(d, side, True)
+                    pass_window(part, owner, side).start()
+
+    def relay_window(part):
+        for d in range(1, n_col - 1):
+            for side in range(2):
+                take_window(part, d, side, True)
+
+    relay_window(0)
 
     to_relay.wait_recv()
 
@@ -130,18 +150,30 @@
         stay = pltpu.make_async_copy(src, dst, self_sem.at[sub])
         return here, away, stay
 
+    def at_end(own):
+        target = x * 2 + k if own else (1 - x) * 2 + k
+        return jnp.logical_or(target == 0, target == n_col - 1)
+
+    def send_quarters(sub, own, kk):
+        here, away, stay = scatter(sub, own, kk)
+
+        @pl.when(here)
+        def _():
+            stay.start()
+
+        @pl.when(jnp.logical_not(here))
+        def _():
+            away.start()
+
     for sub in range(subs):
-        for own in (True, False):
-            for kk in range(2):
-                here, away, stay = scatter(sub, own, kk)
-
-                @pl.when(here)
-                def _():
-                    stay.start()
-
-                @pl.when(jnp.logical_not(here))
-                def _():
-                    away.start()
+        for last in (True, False):
+            for own in (True, False):
+                @pl.when(at_end(own) if last else jnp.logical_not(at_end(own)))
+                def _():
+                    for kk in range(2):
+                        send_quarters(sub, own, kk)
+
+    send_window(1)
 
     def slot_of(sub, q, owner):
         return col.at[sub, owner, pl.ds(pl.multiple_of(q * BLK, BLK), BLK)]
@@ -199,18 +231,6 @@
                 each(steps[at - 1], forward_piece(sub))
         each(steps[-1], forward_piece(sub))
 
-    first_kept = upper * (win_blocks // 2)
-    first_sent = (1 - upper) * (win_blocks // 2)
-    parent_at = [first_sent + i for i in range(win_blocks // 2)]
-    parent_at += [first_kept + i for i in range(win_blocks // 2)]
-
-    def picked(block_of, index, lanes):
-        total = None
-        for j in range(win_blocks):
-            term = block_of(j) * pick_ref[parent_at[index] * win_blocks + j][:, :lanes]
-            total = term if total is None else total + term
-        return total
-
     def sort_front():
         front_copy.wait()
         for i in range(win_blocks):
@@ -218,50 +238,48 @@
                 lambda j: front[j * BLK:(j + 1) * BLK, :], i, front.shape[1]
             )
 
-    def build_window():
+    def build_window(part):
         for side in range(2):
-            take_window(n_col - 1, side, False)
-        own_window.wait()
-        for i in range(win_blocks):
-            rows = pl.ds(i * BLK, BLK)
-            for owner in range(n_col):
-                high, low = split(
-                    picked(lambda j: win[owner, j * BLK:(j + 1) * BLK, :], i, width)
-                )
-                at = owner * width
-                a_cat[rows, at:at + width] = high
-                a_cat[rows, depth + at:depth + at + width] = high
-                a_cat[rows, 2 * depth + at:2 * depth + at + width] = low
+            take_window(part, n_col - 1, side, False)
+        for owner in range(n_col):
+            high, low = split(win[part, owner])
+            at = owner * width
+            rows = slice(part * keep, (part + 1) * keep)
+            a_cat[rows, at:at + width] = high
+            a_cat[rows, depth + at:depth + at + width] = high
+            a_cat[rows, 2 * depth + at:2 * depth + at + width] = low
 
     tile = 2 * BLK
     tiles = n_row * BLK // tile
 
-    def multiply(sub):
+    def build_columns(sub):
         for q in (pair_row, (1 - x) * 2 + 1 - k):
             for offset in steps:
                 each(offset, lambda owner: arrive(sub, q, owner))
         for owner in range(n_col):
             high, low = split(col[sub, owner])
             at = owner * width
-            b_cat[:, at:at + width] = high
-            b_cat[:, depth + at:depth + at + width] = low
-            b_cat[:, 2 * depth + at:2 * depth + at + width] = high
+            b_cat[sub, :, at:at + width] = high
+            b_cat[sub, :, depth + at:depth + at + width] = low
+            b_cat[sub, :, 2 * depth + at:2 * depth + at + width] = high
+
+    def multiply(sub, part):
+        into = snd if part == 0 else mine_ref
         for t in range(tiles):
-            cols = b_cat[t * tile:(t + 1) * tile, :]
-            for part in range(2):
-                product = lax.dot_general(
-                    a_cat[part * keep:(part + 1) * keep, :], cols,
-                    (((1,), (1,)), ((), ())), preferred_element_type=F32,
+            product = lax.dot_general(
+                a_cat[part * keep:(part + 1) * keep, :], b_cat[sub, t * tile:(t + 1) * tile, :],
+                (((1,), (1,)), ((), ())), preferred_element_type=F32,
+            )
+            for b in range(2):
+                q = t * 2 + b
+                column = (q * subs + sub) * BLK
+                into[sub * n_row + q] = (
+                    front_sorted[part * keep:(part + 1) * keep, column:column + BLK]
+                    - product[:, b * BLK:(b + 1) * BLK]
                 )
-                into = snd if part == 0 else mine_ref
-                for i in range(win_blocks // 2):
-                    for b in range(2):
-                        q = t * 2 + b
-                        column = (q * subs + sub) * BLK
-                        into[sub * n_row + q, i * BLK:(i + 1) * BLK, :] = (
-                            front_sorted[part * keep + i * BLK:part * keep + (i + 1) * BLK, column:column + BLK]
-                            - product[i * BLK:(i + 1) * BLK, b * BLK:(b + 1) * BLK]
-                        )
+
+    def send_sibling(sub):
+        for t in range(tiles):
             sibling(sub, t).start()
 
     def sibling(sub, t):
@@ -271,28 +289,34 @@
         )
 
     sort_front()
-    gather(0)
-    build_window()
     for sub in range(subs):
-        multiply(sub)
-        if sub + 1 < subs:
-            gather(sub + 1)
+        gather(sub)
+        if sub == 0:
+            build_window(0)
+        build_columns(sub)
+        multiply(sub, 0)
+        send_sibling(sub)
+    relay_window(1)
+    build_window(1)
+    for sub in range(subs):
+        multiply(sub, 1)
 
     for sub in range(subs):
         for t in range(tiles):
             sibling(sub, t).wait()
     to_relay.wait_send()
-    for side in range(2):
-        @pl.when(has(side))
-        def _():
-            pass_window(c, side, p_ref.at[pl.ds(0, win_rows)]).wait_send()
-
-        for d in range(1, n_col - 1):
-            owner = c - d if side == 0 else c + d
-
-            @pl.when(jnp.logical_and(from_left(d) if side == 0 else from_right(d), has(side)))
+    for part in range(2):
+        for side in range(2):
+            @pl.when(has(side))
             def _():
-                pass_window(owner, side, win.at[owner]).wait_send()
+                pass_window(part, c, side).wait_send()
+
+            for d in range(1, n_col - 1):
+                owner = c - d if side == 0 else c + d
+
+                @pl.when(jnp.logical_and(from_left(d) if side == 0 else from_right(d), has(side)))
+                def _():
+                    pass_window(part, owner, side).wait_send()
     for sub in range(subs):
         for own in (True, False):
             for kk in range(2):
@@ -310,16 +334,30 @@
             each(offset, settle)
 
 
-def merge_kernel(n_row, subs, blocks, own_ref, other_ref, mine_ref, got_ref, out_ref):
-    out_ref[...] = jnp.zeros_like(out_ref)
+def merge_kernel(n_row, subs, blocks, own_ref, other_ref, mine_hbm, got_hbm, out_ref, got_ref, mine_sem, got_sem):
+    def at(j):
+        return (j % subs) * n_row + j // subs
+
+    def spot(maps, j):
+        return pl.ds(pl.multiple_of(maps[0, j] * BLK, BLK), BLK)
+
+    def bring(j):
+        return pltpu.make_async_copy(got_hbm.at[at(j)], got_ref.at[j], got_sem.at[j])
+
+    def lay(j):
+        return pltpu.make_async_copy(mine_hbm.at[at(j)], out_ref.at[:, spot(own_ref, j)], mine_sem.at[j])
+
     for j in range(blocks):
-        at = (j % subs) * n_row + j // subs
-        spot = pl.ds(pl.multiple_of(own_ref[0, j] * BLK, BLK), BLK)
-        out_ref[:, spot] = mine_ref[at]
+        lay(j).start()
     for j in range(blocks):
-        at = (j % subs) * n_row + j // subs
-        spot = pl.ds(pl.multiple_of(other_ref[0, j] * BLK, BLK), BLK)
-        out_ref[:, spot] = out_ref[:, spot] + got_ref[at]
+        bring(j).start()
+    for j in range(blocks, out_ref.shape[1] // BLK):
+        out_ref[:, spot(own_ref, j)] = jnp.zeros((out_ref.shape[0], BLK), F32)
+    for j in range(blocks):
+        lay(j).wait()
+    for j in range(blocks):
+        bring(j).wait()
+        out_ref[:, spot(other_ref, j)] = out_ref[:, spot(other_ref, j)] + got_ref[j]
 
 
 def body(sizes, panel, block_mask, front_rest, row_maps, col_maps):
@@ -350,19 +388,19 @@
         out_specs=(vmem, vmem),
         scratch_shapes=[
             pltpu.VMEM((local_rows // 2, width), F32),
-            pltpu.VMEM((n_col, win_rows, width), F32),
+            pltpu.VMEM((2, n_col, keep, width), F32),
             pltpu.VMEM((subs, n_col, n_row * BLK, width), F32),
             pltpu.VMEM((win_rows, 3 * n_col * width), BF16),
-            pltpu.VMEM((n_row * BLK, 3 * n_col * width), BF16),
+            pltpu.VMEM((subs, n_row * BLK, 3 * n_col * width), BF16),
             pltpu.VMEM((win_rows, front_cols), F32),
             pltpu.VMEM((win_rows, front_cols), F32),
             pltpu.VMEM((blocks, keep, BLK), F32),
-            dma((2, n_col)), dma((n_col,)),
+            dma((2, 2, n_col)), dma((2, n_col)),
             dma((1,)), dma((1,)),
             dma((subs, 2, 2)), dma((subs, n_row, n_col)),
             dma((subs, n_col, 2)), dma((subs, n_col)),
             dma((subs, n_row // 2)), dma((subs, n_row // 2)),
-            dma((2,)), dma((subs,)),
+            dma((1,)), dma((subs,)),
         ],
         compiler_params=pltpu.CompilerParams(
             collective_id=0, has_side_effects=True, vmem_limit_bytes=40 * 1024 * 1024
@@ -372,8 +410,9 @@
     return pl.pallas_call(
         functools.partial(merge_kernel, n_row, subs, blocks),
         out_shape=jax.ShapeDtypeStruct((keep, parent_cols), F32),
-        in_specs=[smem, smem, vmem, vmem],
+        in_specs=[smem, smem] + [pl.BlockSpec(memory_space=pl.ANY)] * 2,
         out_specs=vmem,
+        scratch_shapes=[pltpu.VMEM((blocks, keep, BLK), F32), dma((blocks,)), dma((blocks,))],
         name="merge",
     )(col_maps, other_cols, mine, got)
 

time: 117 us -> 97.2 us (0.83)
  Pallas kernels: 108 us -> 87.4 us
    pallas_call x1, Pallas kernels: 105 us -> 83.9 us  [body(): pl.pallas_call(functools.partial(update_kernel, n_leaf, n_row, n_col), ou...]
  transfers between devices with their start and end apart: 1 -> 1, of which waited for: 0 -> 0; matrix products, arithmetic and copies ran while one was open for 3% -> 4% of each run, Pallas kernels for 90% -> 87%
where the time goes in v2:
time: 97.2 us; the launch traced here: 96.5 us
  Pallas kernels  87.4 us (90%)
  local copies, waits for them, and re-layouts  3.1 us (3%)
  starting transfers between devices  3 us (3%)
  other arithmetic  2.87 us (3%)
    pallas_call x1, Pallas kernels, body(): pl.pallas_call(functools.partial(update_kernel, n_leaf, n_row, n_col), ou...  83.9 us
    pallas_call x1, Pallas kernels, body(): pl.pallas_call(functools.partial(merge_kernel, n_row, subs, blocks), out_...  3.58 us
    ppermute x1, starting transfers between devices, body(): other_cols = lax.ppermute(col_maps, 'leaf', pairs)  3 us
    unnamed x8, local copies, waits for them, and re-layouts  2.5 us
  transfers between devices with their start and end apart: 1, of which 0 were waited for; matrix products, arithmetic and copies ran while one was open for 4% of the time, Pallas kernels for 87%

profile of v2, /device:TPU:0, one launch (start us, length us, event | category | flops | bytes accessed | tf_op | source)
XLA Modules:
  0.0 96.5 jit_solution(2239523288653870210)
XLA Ops:
  0.0 3.0 %collective-permute-start = (s32[1,12]{1,0:T(1,128)}, s32[1,12]{1,0:T(1,128)S(1)}, u32[]{:S(2)}, u32[]{:S(2)}) collective-permute-start(s32[1,12]{1,0:T(1,128)} %own_ref.1), channel_id=1, source_target_pairs={{0,16},{16,0},{1,17},{17,1},{2,18},{18,2},{3,19},{19,3},{4,20},{20... | collective-permute-start | bytes 152 | tf_op jit(solution)/shard_map/ppermute | solution.py:372
  3.0 0.7 convert_element_type.15
  3.7 0.7 fusion
  4.3 0.1 reshape.24
  4.4 0.1 copy.6
  4.5 0.0 copy-start
  4.5 0.3 mul.11
  4.8 1.5 %bitcast_multiply_fusion.p_ref = f32[1024,256]{1,0:T(8,128)S(1)} fusion(f32[1024,256]{1,0:T(8,128)} %param.5, f32[128,8,2,128]{3,2,1,0:T(2,128)S(1)} %bitcast.5), kind=kLoop, calls=%fused_computation | loop fusion | flops 262144 | bytes 3145728 | tf_op jit(solution)/shard_map/mul | solution.py:375
  6.4 0.1 broadcast_in_dim.2.pick_ref
  6.5 0.0 copy-done
  6.5 83.9 %update.1 = (f32[8,256,128]{2,1,0:T(8,128)S(1)}, f32[8,256,128]{2,1,0:T(8,128)S(1)}) custom-call(f32[16,1,1024]{2,1,0:T(1,128)S(1)} %broadcast_in_dim.2.pick_ref, f32[1024,256]{1,0:T(8,128)S(1)} %bitcast_multiply_fusion.p_ref, f32[512,1024]{1,0:T(8,128)S(1)} %copy-done), custom_call_target="tpu_custom_call" | custom-call | tf_op jit(solution)/shard_map/update/pallas_call | solution.py:384
  90.4 0.0 copy-start.1
  90.4 1.0 %copy-done.1 = f32[8,256,128]{2,1,0:T(8,128)} copy-done((f32[8,256,128]{2,1,0:T(8,128)}, f32[8,256,128]{2,1,0:T(8,128)S(1)}, u32[]{:S(2)}) %copy-start.1) | copy-done | bytes 1048600
  91.3 0.0 copy-start.2
  91.3 1.0 %copy-done.2 = f32[8,256,128]{2,1,0:T(8,128)} copy-done((f32[8,256,128]{2,1,0:T(8,128)}, f32[8,256,128]{2,1,0:T(8,128)S(1)}, u32[]{:S(2)}) %copy-start.2) | copy-done | bytes 1048600
  92.4 0.0 collective-permute-done.other_ref
  92.4 0.0 copy-start.3
  92.4 0.5 copy-done.3
  92.9 3.6 %merge.1 = f32[256,1536]{1,0:T(8,128)} custom-call(s32[1,12]{1,0:T(1,128)} %own_ref.1, s32[1,12]{1,0:T(1,128)} %copy-done.3, f32[8,256,128]{2,1,0:T(8,128)} %copy-done.1, f32[8,256,128]{2,1,0:T(8,128)} %copy-done.2), custom_call_target="tpu_custom_call" | custom-call | tf_op jit(solution)/shard_map/merge/pallas_call | solution.py:410
Async XLA Ops:
  0.0 92.4 %collective-permute-start = (s32[1,12]{1,0:T(1,128)}, s32[1,12]{1,0:T(1,128)S(1)}, u32[]{:S(2)}, u32[]{:S(2)}) collective-permute-start(s32[1,12]{1,0:T(1,128)} %own_ref.1), channel_id=1, source_target_pairs={{0,16},{16,0},{1,17},{17,1},{2,18},{18,2},{3,19},{19,3},{4,20},{20... | collective-permute-start | bytes 152 | tf_op jit(solution)/shard_map/ppermute | solution.py:372
  4.5 2.0 %copy-start = (f32[512,1024]{1,0:T(8,128)S(1)}, f32[512,1024]{1,0:T(8,128)}, u32[]{:S(2)}) copy-start(f32[512,1024]{1,0:T(8,128)} %front_hbm.1) | copy-start | bytes 6291460
  90.4 1.0 %copy-start.1 = (f32[8,256,128]{2,1,0:T(8,128)}, f32[8,256,128]{2,1,0:T(8,128)S(1)}, u32[]{:S(2)}) copy-start(f32[8,256,128]{2,1,0:T(8,128)S(1)} %get-tuple-element.7.mine_hbm) | copy-start | bytes 3145732
  91.3 1.0 %copy-start.2 = (f32[8,256,128]{2,1,0:T(8,128)}, f32[8,256,128]{2,1,0:T(8,128)S(1)}, u32[]{:S(2)}) copy-start(f32[8,256,128]{2,1,0:T(8,128)S(1)} %get-tuple-element.8.got_hbm) | copy-start | bytes 3145732
  92.4 0.5 copy-start.3

commit v3 on v2

--- a/solution.py
+++ b/solution.py
@@ -20,11 +20,11 @@
 
 def update_kernel(
     n_leaf, n_row, n_col,
-    pick_ref, p_ref, front_hbm,
-    mine_ref, got_ref,
-    relay, win, col, a_cat, b_cat, front, front_sorted, snd,
+    pick_ref, flag_ref, cols_ref, panel_ref, front_hbm,
+    mine_ref, got_ref, other_ref,
+    p_ref, relay, win, col, a_cat, b_cat, front, front_sorted, snd,
     win_send, win_recv, rel_send, rel_recv, s1_send, col_recv, s2_send, fwd_send,
-    sib_send, sib_recv, loc_sem, self_sem,
+    sib_send, sib_recv, loc_sem, self_sem, map_send, map_recv,
 ):
     leaf, r, c = lax.axis_index("leaf"), lax.axis_index("row"), lax.axis_index("col")
     x, k = r // 2, r % 2
@@ -64,6 +64,12 @@
             total = term if total is None else total + term
         return total
 
+    for i in range(p_ref.shape[0] // BLK):
+        for b in range(p_ref.shape[1] // BLK):
+            spot = slice(i * BLK, (i + 1) * BLK), slice(b * BLK, (b + 1) * BLK)
+            flag = flag_ref[i:i + 1, b:b + 1].astype(F32)
+            p_ref[spot] = panel_ref[spot] * jnp.broadcast_to(flag, (BLK, BLK))
+
     for i in range(win_blocks):
         win[i * BLK // keep, c, pl.ds(i * BLK % keep, BLK), :] = picked(
             lambda j: p_ref[j * BLK:(j + 1) * BLK, :], i, p_ref.shape[1]
@@ -101,6 +107,8 @@
             def _():
                 pass_window(part, c, side).start()
 
+    other_cols = remote(cols_ref, other_ref, map_send.at[0], map_recv.at[0], other_leaf=sib)
+    other_cols.start()
     send_window(0)
     half = 2 * quarter
     to_relay = remote(
@@ -304,6 +312,7 @@
     for sub in range(subs):
         for t in range(tiles):
             sibling(sub, t).wait()
+    other_cols.wait()
     to_relay.wait_send()
     for part in range(2):
         for side in range(2):
@@ -368,12 +377,6 @@
     blocks = front_cols // BLK
     subs = local_rows // n_row // BLK
     parent_cols = PC // n_col
-    pairs = [(source, source ^ (n_leaf // 2)) for source in range(n_leaf)]
-    other_cols = lax.ppermute(col_maps, "leaf", pairs)
-    flags = block_mask.astype(F32)
-    masked = (
-        panel.reshape(local_rows // BLK, BLK, width // BLK, BLK) * flags[:, None, :, None]
-    ).reshape(local_rows, width)
     win_blocks = win_rows // BLK
     pick = (row_maps == jnp.arange(win_blocks, dtype=row_maps.dtype)[:, None]).astype(F32)
     pick = jnp.broadcast_to(pick.reshape(-1, 1, 1), (win_blocks * win_blocks, 1, front_cols))
@@ -381,12 +384,13 @@
     smem = pl.BlockSpec(memory_space=pltpu.SMEM)
     dma = pltpu.SemaphoreType.DMA
     part = jax.ShapeDtypeStruct((blocks, keep, BLK), F32)
-    mine, got = pl.pallas_call(
+    mine, got, other_cols = pl.pallas_call(
         functools.partial(update_kernel, n_leaf, n_row, n_col),
-        out_shape=(part, part),
-        in_specs=[vmem, vmem, pl.BlockSpec(memory_space=pl.ANY)],
-        out_specs=(vmem, vmem),
+        out_shape=(part, part, jax.ShapeDtypeStruct(col_maps.shape, col_maps.dtype)),
+        in_specs=[vmem] * 4 + [pl.BlockSpec(memory_space=pltpu.HBM)],
+        out_specs=(vmem, vmem, vmem),
         scratch_shapes=[
+            pltpu.VMEM((local_rows, width), F32),
             pltpu.VMEM((local_rows // 2, width), F32),
             pltpu.VMEM((2, n_col, keep, width), F32),
             pltpu.VMEM((subs, n_col, n_row * BLK, width), F32),
@@ -400,19 +404,20 @@
             dma((subs, 2, 2)), dma((subs, n_row, n_col)),
             dma((subs, n_col, 2)), dma((subs, n_col)),
             dma((subs, n_row // 2)), dma((subs, n_row // 2)),
-            dma((1,)), dma((subs,)),
+            dma((1,)), dma((subs,)), dma((1,)), dma((1,)),
         ],
         compiler_params=pltpu.CompilerParams(
             collective_id=0, has_side_effects=True, vmem_limit_bytes=40 * 1024 * 1024
         ),
         name="update",
-    )(pick, masked, front_rest)
+    )(pick, block_mask, col_maps, panel, front_rest)
     return pl.pallas_call(
         functools.partial(merge_kernel, n_row, subs, blocks),
         out_shape=jax.ShapeDtypeStruct((keep, parent_cols), F32),
         in_specs=[smem, smem] + [pl.BlockSpec(memory_space=pl.ANY)] * 2,
         out_specs=vmem,
         scratch_shapes=[pltpu.VMEM((blocks, keep, BLK), F32), dma((blocks,)), dma((blocks,))],
+        compiler_params=pltpu.CompilerParams(vmem_limit_bytes=8 * 1024 * 1024),
         name="merge",
     )(col_maps, other_cols, mine, got)
 

time: 97.2 us -> 96 us (0.988)
  starting transfers between devices: 3 us -> 0 us
  Pallas kernels: 87.4 us -> 90.1 us
  other arithmetic: 2.87 us -> 0.66 us
  local copies, waits for them, and re-layouts: 3.1 us -> 4.4 us
    ppermute x1 -> x0, starting transfers between devices: 3 us -> none  [body(): other_cols = lax.ppermute(col_maps, 'leaf', pairs)]
    pallas_call x1, Pallas kernels: 83.9 us -> 86.5 us  [body(): pl.pallas_call(functools.partial(update_kernel, n_leaf, n_row, n_col), ou...]
    unnamed x8 -> x7, local copies, waits for them, and re-layouts: 2.5 us -> 4.22 us
    mul x1 -> x0, other arithmetic: 1.53 us -> none  [body(): panel.reshape(local_rows // BLK, BLK, width // BLK, BLK)]
  transfers between devices with their start and end apart: 1 -> 0, of which waited for: 0 -> 0; matrix products, arithmetic and copies ran while one was open for 4% -> 0% of each run, Pallas kernels for 87% -> 0%
where the time goes in v3:
time: 96 us; the launch traced here: 95.2 us
  Pallas kernels  90.1 us (94%)
  local copies, waits for them, and re-layouts  4.4 us (5%)
    pallas_call x1, Pallas kernels, body(): pl.pallas_call(functools.partial(update_kernel, n_leaf, n_row, n_col), ou...  86.5 us
    unnamed x7, local copies, waits for them, and re-layouts  4.22 us
    pallas_call x1, Pallas kernels, body(): pl.pallas_call(functools.partial(merge_kernel, n_row, subs, blocks), out_...  3.6 us

profile of v3, /device:TPU:0, one launch (start us, length us, event | category | flops | bytes accessed | tf_op | source)
XLA Modules:
  0.0 95.2 jit_solution(16086351627073581954)
XLA Ops:
  0.0 0.7 fusion
  0.7 0.1 reshape.20
  0.7 0.8 copy.6.flag_ref
  1.5 0.1 broadcast_in_dim.2.pick_ref
  1.6 0.0 copy-start
  1.6 1.6 %copy-done = f32[512,1024]{1,0:T(8,128)S(1)} copy-done((f32[512,1024]{1,0:T(8,128)S(1)}, f32[512,1024]{1,0:T(8,128)}, u32[]{:S(2)}) %copy-start) | copy-done | bytes 2097176
  3.2 0.0 copy-start.1
  3.2 1.2 %copy-done.1 = f32[1024,256]{1,0:T(8,128)S(1)} copy-done((f32[1024,256]{1,0:T(8,128)S(1)}, f32[1024,256]{1,0:T(8,128)}, u32[]{:S(2)}) %copy-start.1) | copy-done | bytes 1048600
  4.4 0.0 copy-start.2
  4.4 0.7 copy-done.2
  5.1 86.5 %update.1 = (f32[8,256,128]{2,1,0:T(8,128)S(1)}, f32[8,256,128]{2,1,0:T(8,128)S(1)}, s32[1,12]{1,0:T(1,128)S(1)}) custom-call(f32[16,1,1024]{2,1,0:T(1,128)S(1)} %broadcast_in_dim.2.pick_ref, s32[8,2]{1,0:T(8,128)S(1)} %copy.6.flag_ref, s32[1,12]{1,0:T(1,128)S(1)} %copy-done.2, f32[1024,256]{1,0:T(8,128)S(1)} %copy-done.1, f32[512,1024]{1,0:T(8,128)S(1)} %copy-done), custom_call_target="tpu_custom_call" | custom-call | tf_op jit(solution)/shard_map/update/pallas_call | solution.py:387
  91.6 3.6 %merge.1 = f32[256,1536]{1,0:T(8,128)} custom-call(s32[1,12]{1,0:T(1,128)S(1)} %copy-done.2, s32[1,12]{1,0:T(1,128)S(1)} %get-tuple-element.8.other_ref, f32[8,256,128]{2,1,0:T(8,128)S(1)} %get-tuple-element.9.mine_hbm, f32[8,256,128]{2,1,0:T(8,128)S(1)} %get-tuple-element.10.got_hbm), custom_call_target="tpu_custom_call" | custom-call | tf_op jit(solution)/shard_map/merge/pallas_call | solution.py:414
Async XLA Ops:
  1.6 1.6 %copy-start = (f32[512,1024]{1,0:T(8,128)S(1)}, f32[512,1024]{1,0:T(8,128)}, u32[]{:S(2)}) copy-start(f32[512,1024]{1,0:T(8,128)} %front_hbm.1) | copy-start | bytes 6291460
  3.2 1.2 %copy-start.1 = (f32[1024,256]{1,0:T(8,128)S(1)}, f32[1024,256]{1,0:T(8,128)}, u32[]{:S(2)}) copy-start(f32[1024,256]{1,0:T(8,128)} %panel_ref.1) | copy-start | bytes 3145732
  4.4 0.7 copy-start.2
